TPU v7x, 32 devices: a whole 2x2x4 slice. The times are simulated.
32 devices in a mesh: dp: 32 (over z, y, x, core).
Axes of the slice: x: 2, y: 2, z: 4, core: 2. Of those that a mesh axis runs over, the one named last changes fastest.
Arguments:
- images: bfloat16 [256, 196, 512], P('dp'), may hold values from -6 to 6
- cotangent: bfloat16 [256, 196, 512], P('dp'), may hold values from -6 to 6
- image_counts: int32 [32], P('dp'), may hold values from 1 to 8, as said below
- shift_mask: int32 [4, 49, 49], replicated, may hold values from 0 to 1, as said below
- rel_index: int32 [49, 49], replicated, may hold values from 0 to 168
- step_count: int32 [1], replicated, may hold values from 1 to 20
- attend_weight: bfloat16 [512, 1536], P('dp'), may hold values from -0.25 to 0.25
- merge_weight: bfloat16 [512, 512], P('dp'), may hold values from -1 to 1
- expand_weight: bfloat16 [512, 2048], P('dp'), may hold values from -0.25 to 0.25
- project_weight: bfloat16 [2048, 512], P('dp'), may hold values from -0.125 to 0.125
- norm_gains: float32 [2, 512], replicated, may hold values from 0.1 to 1.9
- norm_shifts: float32 [2, 512], replicated, may hold values from -2 to 2
- layer_biases: float32 [4608], replicated, may hold values from -2 to 2
- bias_table: float32 [169, 16], replicated, may hold values from -4 to 4
- attend_momentum: float32 [512, 1536], P('dp'), may hold values from -1.2 to 1.2
- merge_momentum: float32 [512, 512], P('dp'), may hold values from -1.2 to 1.2
- expand_momentum: float32 [512, 2048], P('dp'), may hold values from -1.2 to 1.2
- project_momentum: float32 [2048, 512], P('dp'), may hold values from -1.2 to 1.2
- gains_mean: float32 [2, 512], replicated, may hold values from -0.6 to 0.6
- gains_square: float32 [2, 512], replicated, may hold values from 0.0001 to 0.001
- shifts_mean: float32 [2, 512], replicated, may hold values from -0.6 to 0.6
- shifts_square: float32 [2, 512], replicated, may hold values from 0.0001 to 0.001
- biases_mean: float32 [4608], replicated, may hold values from -0.6 to 0.6
- biases_square: float32 [4608], replicated, may hold values from 0.0001 to 0.001
- table_mean: float32 [169, 16], replicated, may hold values from -0.6 to 0.6
- table_square: float32 [169, 16], replicated, may hold values from 0.0001 to 0.001
Outputs:
- block_out: bfloat16 [256, 196, 512], P('dp')
- input_grad: float32 [256, 196, 512], P('dp')
- attend_grad: float32 [512, 1536], P('dp')
- attend_momentum_next: float32 [512, 1536], P('dp')
- attend_update: float32 [512, 1536], P('dp')
- merge_grad: float32 [512, 512], P('dp')
- merge_momentum_next: float32 [512, 512], P('dp')
- merge_update: float32 [512, 512], P('dp')
- expand_grad: float32 [512, 2048], P('dp')
- expand_momentum_next: float32 [512, 2048], P('dp')
- expand_update: float32 [512, 2048], P('dp')
- project_grad: float32 [2048, 512], P('dp')
- project_momentum_next: float32 [2048, 512], P('dp')
- project_update: float32 [2048, 512], P('dp')
- gains_grad: float32 [2, 512], replicated
- gains_mean_next: float32 [2, 512], replicated
- gains_square_next: float32 [2, 512], replicated
- gains_update: float32 [2, 512], replicated
- shifts_grad: float32 [2, 512], replicated
- shifts_mean_next: float32 [2, 512], replicated
- shifts_square_next: float32 [2, 512], replicated
- shifts_update: float32 [2, 512], replicated
- biases_grad: float32 [4608], replicated
- biases_mean_next: float32 [4608], replicated
- biases_square_next: float32 [4608], replicated
- biases_update: float32 [4608], replicated
- table_grad: float32 [169, 16], replicated
- table_mean_next: float32 [169, 16], replicated
- table_square_next: float32 [169, 16], replicated
- table_update: float32 [169, 16], replicated
Inputs may be any that keep to these rules, and one draw needn't show every extreme that they name: `image_counts`: one device holds 8 live images and another holds 1; live images fill a device's first slots. `shift_mask`: 1 where two patches of a window may attend to each other; symmetric, with ones on the diagonal.
All inputs are finite; a program needn't handle non-finite values.
Results may differ from a plain program's by a relative error of at most 0.0095.
The roundings to bfloat16 on the way count: a program that leaves them out, or rounds other values in their place, can miss the bound.
Values may be sent and summed in bfloat16 or wider, within the bound.
No kernel may reach another device: no remote copies, remote signals or barrier semaphores. Data moves between devices by JAX's collectives and lax.ppermute only.
A program may use at most 256 MiB of HBM per device.

v0:
```python
from functools import partial
import math

import jax
import jax.numpy as jnp
from jax import lax
from jax.sharding import PartitionSpec as P

HEADS = 16
WIN = 7
SIDE = 14
SHIFT = 3
WIN_TOK = 49
PATCHES = 196
TABLE = 169


highest = lax.Precision.HIGHEST
newton_first = 3.4445
newton_second = -4.775
newton_third = 2.0315


def as_sent(shard):

    def short(part):
        return part.astype(jnp.bfloat16) if part.dtype == jnp.float32 else part

    return jax.tree.map(short, shard)


def layer_norm(values, gain, shift):
    center = values - jnp.mean(values, axis=-1, keepdims=True)
    spread = jnp.mean(center * center, axis=-1, keepdims=True)
    return center * lax.rsqrt(spread + 1e-05) * gain + shift


def gelu_exact(values):
    return jax.nn.gelu(values, approximate=False)


def to_windows(field):
    count = field.shape[0]
    blocks = SIDE // WIN
    square = field.reshape(count, SIDE, SIDE, field.shape[-1])
    rolled = jnp.roll(square, (-SHIFT, -SHIFT), (1, 2))
    parted = rolled.reshape(count, blocks, WIN, blocks, WIN, field.shape[-1])
    return parted.transpose(0, 1, 3, 2, 4, 5).reshape(
        count * blocks * blocks, WIN * WIN, field.shape[-1]
    )


def from_windows(windows, count):
    blocks = SIDE // WIN
    parted = windows.reshape(count, blocks, blocks, WIN, WIN, windows.shape[-1])
    square = parted.transpose(0, 1, 3, 2, 4, 5).reshape(count, SIDE, SIDE, windows.shape[-1])
    return jnp.roll(square, (SHIFT, SHIFT), (1, 2)).reshape(count, SIDE * SIDE, windows.shape[-1])


def split_heads(rows):
    return rows.reshape(rows.shape[0], rows.shape[1], HEADS, -1).transpose(0, 2, 1, 3)


def merge_heads(rows):
    return rows.transpose(0, 2, 1, 3).reshape(rows.shape[0], rows.shape[2], -1)


def orthogonalize(matrix):
    tall = matrix.shape[0] > matrix.shape[1]
    current = matrix.T if tall else matrix
    current = current / (jnp.sqrt(jnp.sum(current * current)) + 1e-07)
    for sweep in range(5):
        square = jnp.dot(current, current.T, precision=highest)
        mixer = newton_second * square + newton_third * jnp.dot(square, square, precision=highest)
        current = newton_first * current + jnp.dot(mixer, current, precision=highest)
    return current.T if tall else current


def adamw_step(param, grad, first, second, steps):
    first_next = 0.9 * first + 0.1 * grad
    second_next = 0.999 * second + 0.001 * grad * grad
    first_hat = first_next / (1.0 - jnp.power(0.9, steps))
    second_hat = second_next / (1.0 - jnp.power(0.999, steps))
    update = -0.05 * (first_hat / (jnp.sqrt(second_hat) + 1e-08) + 0.05 * param)
    return (first_next, second_next, update)


def padded_rows(flat, length):
    return jnp.pad(flat, ((0, 0), (0, length - flat.shape[1])))


def local(
    images,
    cotangent,
    image_counts,
    shift_mask,
    rel_index,
    step_count,
    attend_weight,
    merge_weight,
    expand_weight,
    project_weight,
    norm_gains,
    norm_shifts,
    layer_biases,
    bias_table,
    attend_momentum,
    merge_momentum,
    expand_momentum,
    project_momentum,
    gains_mean,
    gains_square,
    shifts_mean,
    shifts_square,
    biases_mean,
    biases_square,
    table_mean,
    table_square,
):
    f32 = jnp.float32
    bf16 = jnp.bfloat16
    slots = images.shape[0]
    width = images.shape[2]
    devices = lax.axis_size("dp")
    hidden_units = expand_weight.shape[1]
    scale = 1.0 / math.sqrt(width // HEADS)
    grad_scale = 1.0 / math.sqrt(slots * devices * PATCHES)
    gathered = (
        lax.all_gather(attend_weight, "dp", axis=0, tiled=True),
        lax.all_gather(merge_weight, "dp", axis=0, tiled=True),
        lax.all_gather(expand_weight, "dp", axis=0, tiled=True),
        lax.all_gather(project_weight, "dp", axis=0, tiled=True),
    )
    attend_full, merge_full, expand_full, project_full = gathered
    valid = (jnp.arange(slots) < image_counts[0]).astype(f32)[:, None, None]
    mask_add = -100.0 * (1 - shift_mask).astype(f32)
    masking = jnp.tile(mask_add, (slots, 1, 1))[:, None]
    one_hot = (rel_index.reshape(-1)[:, None] == jnp.arange(TABLE)[None, :]).astype(f32)
    position = jnp.dot(one_hot, bias_table, precision=highest).T.reshape(HEADS, WIN_TOK, WIN_TOK)
    features = images.astype(f32)
    normed, norm_pull = jax.vjp(layer_norm, features, norm_gains[0], norm_shifts[0])
    windows = to_windows(normed.astype(bf16))
    triple = (
        jnp.einsum("wtd,de->wte", windows, attend_full, preferred_element_type=f32)
        + layer_biases[: 3 * width]
    )
    queries = split_heads(triple[..., :width] * scale).astype(bf16)
    keys_low = split_heads(triple[..., width : 2 * width]).astype(bf16)
    values_low = split_heads(triple[..., 2 * width :]).astype(bf16)
    scores = (
        jnp.einsum("whqc,whkc->whqk", queries, keys_low, preferred_element_type=f32)
        + position
        + masking
    )
    attention = jax.nn.softmax(scores, axis=-1)
    attention_low = attention.astype(bf16)
    mixed = merge_heads(
        jnp.einsum("whqk,whkc->whqc", attention_low, values_low, preferred_element_type=f32)
    ).astype(bf16)
    branch = (
        jnp.einsum("wtd,de->wte", mixed, merge_full, preferred_element_type=f32)
        + layer_biases[3 * width : 4 * width]
    )
    middle = features + from_windows(branch, slots)
    normed_two, norm_two_pull = jax.vjp(layer_norm, middle, norm_gains[1], norm_shifts[1])
    normed_low = normed_two.astype(bf16)
    pre_act = (
        jnp.einsum("itd,df->itf", normed_low, expand_full, preferred_element_type=f32)
        + layer_biases[4 * width : 4 * width + hidden_units]
    )
    activated, gelu_pull = jax.vjp(gelu_exact, pre_act)
    active_low = activated.astype(bf16)
    mlp_out = (
        jnp.einsum("itf,fd->itd", active_low, project_full, preferred_element_type=f32)
        + layer_biases[4 * width + hidden_units :]
    )
    block_out = (valid * (middle + mlp_out)).astype(bf16)
    attend_back, merge_back, expand_back, project_back = (
        lax.all_gather(attend_weight, "dp", axis=0, tiled=True),
        lax.all_gather(merge_weight, "dp", axis=0, tiled=True),
        lax.all_gather(expand_weight, "dp", axis=0, tiled=True),
        lax.all_gather(project_weight, "dp", axis=0, tiled=True),
    )
    grad_out = valid * cotangent.astype(f32)
    grad_out_low = grad_out.astype(bf16)
    project_term = jnp.einsum("itf,itd->fd", active_low, grad_out_low, preferred_element_type=f32)
    grad_act = jnp.einsum("itd,fd->itf", grad_out_low, project_back, preferred_element_type=f32)
    grad_pre = gelu_pull(grad_act)[0].astype(bf16)
    expand_term = jnp.einsum("itd,itf->df", normed_low, grad_pre, preferred_element_type=f32)
    grad_normed_two = jnp.einsum("itf,df->itd", grad_pre, expand_back, preferred_element_type=f32)
    grad_mid_norm, gain_two, shift_two = norm_two_pull(grad_normed_two)
    grad_middle = grad_out + grad_mid_norm
    grad_branch = to_windows(grad_middle).astype(bf16)
    merge_term = jnp.einsum("wtd,wte->de", mixed, grad_branch, preferred_element_type=f32)
    grad_mixed = split_heads(
        jnp.einsum("wte,de->wtd", grad_branch, merge_back, preferred_element_type=f32).astype(bf16)
    )
    grad_values = jnp.einsum(
        "whqk,whqc->whkc", attention_low, grad_mixed, preferred_element_type=f32
    )
    grad_attention = jnp.einsum(
        "whqc,whkc->whqk", grad_mixed, values_low, preferred_element_type=f32
    )
    grad_scores = (
        attention * (grad_attention - jnp.sum(grad_attention * attention, axis=-1, keepdims=True))
    ).astype(bf16)
    position_grad = jnp.sum(grad_scores, axis=0, dtype=f32).reshape(HEADS, WIN_TOK * WIN_TOK)
    table_term = jnp.dot(one_hot.T, position_grad.T, precision=highest)
    grad_queries = jnp.einsum("whqk,whkc->whqc", grad_scores, keys_low, preferred_element_type=f32)
    grad_keys = jnp.einsum("whqk,whqc->whkc", grad_scores, queries, preferred_element_type=f32)
    grad_triple = jnp.concatenate(
        [merge_heads(grad_queries) * scale, merge_heads(grad_keys), merge_heads(grad_values)],
        axis=-1,
    ).astype(bf16)
    attend_term = jnp.einsum("wtd,wte->de", windows, grad_triple, preferred_element_type=f32)
    grad_normed = from_windows(
        jnp.einsum("wte,de->wtd", grad_triple, attend_back, preferred_element_type=f32), slots
    )
    grad_feat, gain_one, shift_one = norm_pull(grad_normed)
    input_grad = grad_middle + grad_feat
    bias_term = jnp.concatenate(
        [
            jnp.sum(grad_triple, axis=(0, 1), dtype=f32),
            jnp.sum(grad_branch, axis=(0, 1), dtype=f32),
            jnp.sum(grad_pre, axis=(0, 1), dtype=f32),
            jnp.sum(grad_out_low, axis=(0, 1), dtype=f32),
        ]
    )
    mat_sums = (
        lax.psum_scatter(attend_term, "dp", scatter_dimension=0, tiled=True),
        lax.psum_scatter(merge_term, "dp", scatter_dimension=0, tiled=True),
        lax.psum_scatter(expand_term, "dp", scatter_dimension=0, tiled=True),
        lax.psum_scatter(project_term, "dp", scatter_dimension=0, tiled=True),
    )
    small_sums = lax.psum(
        (jnp.stack([gain_one, gain_two]), jnp.stack([shift_one, shift_two]), bias_term, table_term),
        "dp",
    )
    mat_grads = tuple((term * grad_scale for term in mat_sums))
    small_grads = tuple((term * grad_scale for term in small_sums))
    momenta = (attend_momentum, merge_momentum, expand_momentum, project_momentum)
    momenta_next = tuple((0.95 * moment + grad for moment, grad in zip(momenta, mat_grads)))
    stride = 1
    owner_ranks = [order * stride for order in range(4)]
    rank_index = lax.axis_index("dp")
    shard_sizes = [moment.size for moment in momenta_next]
    longest = max(shard_sizes)
    whole = lax.all_gather(momenta_next, "dp", axis=0, tiled=True)
    owner_terms = tuple(
        (
            lax.cond(
                rank_index == owner_ranks[order],
                partial(orthogonalize, matrix),
                partial(jnp.zeros_like, matrix),
            )
            for order, matrix in enumerate(whole)
        )
    )
    packed = jnp.zeros((devices, longest), f32)
    for order, term in enumerate(owner_terms):
        packed = packed + padded_rows(term.reshape(devices, shard_sizes[order]), longest)
    received = lax.all_to_all(
        as_sent(packed), "dp", split_axis=0, concat_axis=0, tiled=True
    ).astype(packed.dtype)
    orth_rows = tuple(
        (
            received[owner_ranks[order], : shard_sizes[order]].reshape(moment.shape)
            for order, moment in enumerate(momenta_next)
        )
    )
    results = [block_out, input_grad]
    for grad, moment_next, orth_part, matrix in zip(mat_grads, momenta_next, orth_rows, whole):
        update = -0.02 * math.sqrt(max(matrix.shape)) * orth_part
        results += [grad, moment_next, update]
    steps = step_count[0].astype(f32)
    params = (norm_gains, norm_shifts, layer_biases, bias_table)
    states = (
        (gains_mean, gains_square),
        (shifts_mean, shifts_square),
        (biases_mean, biases_square),
        (table_mean, table_square),
    )
    for param, grad, state in zip(params, small_grads, states):
        first_next, second_next, update = adamw_step(param, grad, state[0], state[1], steps)
        results += [grad, first_next, second_next, update]
    return tuple(results)


def solution(mesh):
    return jax.shard_map(
        local,
        mesh=mesh,
        in_specs=(
            P("dp", None, None),
            P("dp", None, None),
            P("dp"),
            P(),
            P(),
            P(),
            P("dp", None),
            P("dp", None),
            P("dp", None),
            P("dp", None),
            P(),
            P(),
            P(),
            P(),
            P("dp", None),
            P("dp", None),
            P("dp", None),
            P("dp", None),
            P(),
            P(),
            P(),
            P(),
            P(),
            P(),
            P(),
            P(),
        ),
        out_specs=(
            P("dp", None, None),
            P("dp", None, None),
            P("dp", None),
            P("dp", None),
            P("dp", None),
            P("dp", None),
            P("dp", None),
            P("dp", None),
            P("dp", None),
            P("dp", None),
            P("dp", None),
            P("dp", None),
            P("dp", None),
            P("dp", None),
            P(),
            P(),
            P(),
            P(),
            P(),
            P(),
            P(),
            P(),
            P(),
            P(),
            P(),
            P(),
            P(),
            P(),
            P(),
            P(),
        ),
        check_vma=False,
    )
```

profile of v0, /device:TPU:0, one launch (start us, length us, event | category | flops | bytes accessed | tf_op | source)
XLA Modules:
  0.0 1322.5 jit_solution(11692982071132868505)
XLA Ops:
  25.4 47.9 %all_gather.41 = bf16[512,512]{1,0:T(8,128)(2,1)} all-gather(bf16[16,512]{1,0:T(8,128)(2,1)S(1)} %copy-done.51), channel_id=1, replica_groups=mesh['dp'=32] {'dp'}, dimensions={0}, use_global_device_ids=true | all-gather | bytes 540672 | tf_op jit(solution)/shard_map/all_gather | solution.py:130
  95.0 11.8 fusion.125
  106.8 7.9 fusion.76
  136.5 9.2 fusion.68
  150.3 31.3 %multiply_convert_fusion.1 = (bf16[8,196,2048]{2,1,0:T(8,128)(2,1)}, f32[8,196,2048]{2,1,0:T(8,128)}) fusion(f32[8,196,2048]{2,1,0:T(8,128)S(1)} %get-tuple-element.268, f32[2048]{0:T(1024)S(1)} %copy-done.46, u8[196,2048]{1,0:T(8,128)(4,1)S(1)} %get-tuple-element.201, u8[196,2048]{1,0:T(8,128)(4,1)S(1)} %get-tuple-element.200), kind=kLoop, calls=%fused_computation.103 | loop fusion | flops 227999744 | bytes 32923648 | tf_op jit(solution)/shard_map/convert_element_type | solution.py:172
  185.9 18.7 %convert_reduce_fusion.1 = (f32[2048]{0:T(1024)}, bf16[8,196,2048]{2,1,0:T(8,128)(2,1)}) fusion(f32[8,196,2048]{2,1,0:T(8,128)} %get-tuple-element.249, bf16[2048,512]{1,0:T(8,128)(2,1)} %all-gather.12.cloned.1.call-done, f32[8]{0:T(128)} %compare_convert_fusion, bf16[8,196,512]{2,0,1:T(8,128)(2,1)} %param.35, f32[8,196,2048]{2,1,0:T(8,128)} %copy-done.10, ...), kind=kOutput, calls=%fused_computation.101 | convolution fusion | flops 3345332224 | bytes 35831840 | tf_op jit(solution)/shard_map/itd,fd->itf/dot_general | solution.py:187
  231.1 8.1 reshape.282
  239.2 10.5 copy.230
  249.7 13.1 multiply_reduce_fusion.4
  262.8 14.6 %convert_reduce_fusion = (f32[16,49,49]{1,2,0:T(8,128)}, bf16[32,16,49,49]{2,3,1,0:T(8,128)(2,1)}) fusion(f32[32,16,49,49]{2,3,1,0:T(8,128)} %get-tuple-element.271, f32[32,16,49]{2,1,0:T(8,128)S(1)} %get-tuple-element.270, f32[32,16,49,49]{2,3,1,0:T(8,128)} %get-tuple-element.267, f32[32,16,49]{2,1,0:T(8,128)S(1)} %get-tuple-element.266), kind=kLoop, calls=%fused_computation.90 | loop fusion | flops 7337456 | bytes 12647488 | tf_op jit(solution)/shard_map/reduce_sum | solution.py:207
  277.4 8.5 multiply_convert_fusion.2
  285.9 10.3 convolution_convert_fusion
  296.2 8.8 fusion.79
  334.6 9.1 convolution_bitcast_fusion.2
  345.2 9.3 convolution_bitcast_fusion.1
  354.6 101.2 %reduce-scatter.7.cloned.1.call-done = f32[16,512]{1,0:T(8,128)} async-done(((f32[512,512]{1,0:T(8,128)}), f32[16,512]{1,0:T(8,128)}) %reduce-scatter.7.cloned.1.call-update) | async-done | bytes 32784 | tf_op jit(solution)/shard_map/reduce_scatter | solution.py:231
  457.3 102.7 %reduce-scatter.5.cloned.1.call-done = f32[16,1536]{1,0:T(8,128)} async-done(((f32[512,1536]{1,0:T(8,128)}), f32[16,1536]{1,0:T(8,128)}) %reduce-scatter.5.cloned.1.call-update) | async-done | bytes 98320 | tf_op jit(solution)/shard_map/reduce_scatter | solution.py:230
  561.7 140.6 %reduce-scatter.9.cloned.1.call-done = f32[16,2048]{1,0:T(8,128)} async-done(((f32[512,2048]{1,0:T(8,128)}), f32[16,2048]{1,0:T(8,128)}) %reduce-scatter.9.cloned.1.call-update) | async-done | bytes 131088 | tf_op jit(solution)/shard_map/reduce_scatter | solution.py:232
  704.4 137.2 %reduce-scatter.11.cloned.1.call-done = f32[64,512]{1,0:T(8,128)} async-done(((f32[2048,512]{1,0:T(8,128)}), f32[64,512]{1,0:T(8,128)}) %reduce-scatter.11.cloned.1.call-update) | async-done | bytes 131088 | tf_op jit(solution)/shard_map/reduce_scatter | solution.py:233
  844.0 7.0 fusion.51
  863.7 31.3 %all-gather.16.cloned.1.call-done = f32[512,512]{1,0:T(8,128)} async-done(((f32[16,512]{1,0:T(8,128)}), f32[512,512]{1,0:T(8,128)}) %all-gather.16.cloned.1.call-update) | async-done | bytes 1048592 | tf_op jit(solution)/shard_map/all_gather | solution.py:248
  895.0 11.3 conditional.5
  906.3 50.5 %all-gather.14.cloned.1.call-done = f32[512,1536]{1,0:T(8,128)} async-done(((f32[16,1536]{1,0:T(8,128)}), f32[512,1536]{1,0:T(8,128)}) %all-gather.14.cloned.1.call-update) | async-done | bytes 3145744 | tf_op jit(solution)/shard_map/all_gather | solution.py:248
  956.8 77.7 %conditional.4 = (f32[32,32768]{1,0:T(8,128)}) conditional(s32[]{:T(128)} %convert_element_type.166, () %tuple.40, f32[512,1536]{1,0:T(8,128)} %all-gather.14.cloned.1.call-done), branch_computations={%region_12.13_spmd, %region_13.15_spmd} | conditional | flops 56387174400 | bytes 97517640 | solution.py:251
  960.8 8.3 fusion.5
  1034.5 12.3 conditional.6
  1046.8 39.0 %all-gather.20.cloned.1.call-done = f32[2048,512]{1,0:T(8,128)} async-done(((f32[64,512]{1,0:T(8,128)}), f32[2048,512]{1,0:T(8,128)}) %all-gather.20.cloned.1.call-update) | async-done | bytes 4194320 | tf_op jit(solution)/shard_map/all_gather | solution.py:248
  1085.9 8.3 conditional.7
  1108.8 106.6 %all-to-all-start = ((bf16[32,2,16384]{2,1,0:T(2,128)(2,1)}), bf16[32,2,16384]{2,1,0:T(2,128)(2,1)}, u32[]{:S(2)}, u32[]{:S(2)}) async-start(bf16[32,2,16384]{2,1,0:T(2,128)(2,1)} %reshape.321), calls=%async_computation.4 | async-start | bytes 4194304 | tf_op jit(solution)/shard_map/all_to_all | solution.py:262
  1238.1 46.8 %all-reduce.4 = (f32[2,512]{1,0:T(2,128)S(1)}, f32[2,512]{1,0:T(2,128)S(1)}, f32[4608]{0:T(1024)S(1)}, f32[169,16]{0,1:T(8,128)S(1)}) all-reduce(f32[2,512]{1,0:T(2,128)S(1)} %pad_maximum_fusion.9, f32[2,512]{1,0:T(2,128)S(1)} %pad_maximum_fusion.10, f32[4608]{0:T(1024)S(1)} %pad_maximum_fusion.8, ...), channel_id=1, replica_groups=mesh['dp'=32] {'dp'}, use_global_device_ids=true, to_apply=%region_29.30 | all-reduce | flops 9360 | bytes 74880 | tf_op jit(solution)/shard_map/psum | solution.py:235
  1287.0 10.5 reshape.322
  1297.4 11.1 convert_element_type.171
  (310 shorter events, 267.8 us)
Async XLA Ops:
  7.2 67.3 %all-gather.8.cloned.1.call-start = ((), (), s32[]{:S(2)}) async-start(), calls=%async_computation.5 | async-start | bytes 1622016 | tf_op jit(solution)/shard_map/all_gather | solution.py:129
  7.9 128.6 %all-gather.10.cloned.1.call-start = ((), (), s32[]{:S(2)}) async-start(), calls=%async_computation.6 | async-start | bytes 2162688 | tf_op jit(solution)/shard_map/all_gather | solution.py:131
  8.7 177.2 %all-gather.12.cloned.1.call-start = ((), (), s32[]{:S(2)}) async-start(), calls=%async_computation.7 | async-start | bytes 2162688 | tf_op jit(solution)/shard_map/all_gather | solution.py:132
  9.4 446.4 %reduce-scatter.7.cloned.1.call-start = ((), (), s32[]{:S(2)}) async-start(), calls=%async_computation.10 | async-start | bytes 1081344 | tf_op jit(solution)/shard_map/reduce_scatter | solution.py:231
  20.3 54.2 %slice-start.2 = ((f32[4608]{0:T(1024)}), f32[1536]{0:T(1024)S(1)}, s32[]{:S(2)}) async-start(f32[4608]{0:T(1024)} %param.46), calls=%async_computation.18 | async-start | bytes 16384 | tf_op jit(solution)/shard_map/slice | solution.py:145
  22.6 58.5 %copy-start.19 = (bf16[32,49,512]{2,0,1:T(8,128)(2,1)}, bf16[32,49,512]{2,0,1:T(8,128)(2,1)S(1)}, u32[]{:S(2)}) copy-start(bf16[32,49,512]{2,0,1:T(8,128)(2,1)S(1)} %reshape.277) | copy-start | bytes 4816900
  134.8 199.7 %copy-start = (f32[8,196,512]{2,1,0:T(8,128)}, f32[8,196,512]{2,1,0:T(8,128)S(1)}, u32[]{:S(2)}) copy-start(f32[8,196,512]{2,1,0:T(8,128)S(1)} %get-tuple-element.251) | copy-start | bytes 9633796
  322.0 238.0 %reduce-scatter.5.cloned.1.call-start = ((), (), s32[]{:S(2)}) async-start(), calls=%async_computation.8 | async-start | bytes 3244032 | tf_op jit(solution)/shard_map/reduce_scatter | solution.py:230
  334.5 367.8 %reduce-scatter.9.cloned.1.call-start = ((), (), s32[]{:S(2)}) async-start(), calls=%async_computation.12 | async-start | bytes 4325376 | tf_op jit(solution)/shard_map/reduce_scatter | solution.py:232
  343.8 497.8 %reduce-scatter.11.cloned.1.call-start = ((), (), s32[]{:S(2)}) async-start(), calls=%async_computation.14 | async-start | bytes 4325376 | tf_op jit(solution)/shard_map/reduce_scatter | solution.py:233
  354.5 101.3 %copy-start.45 = (f32[16,512]{1,0:T(8,128)S(1)}, f32[16,512]{1,0:T(8,128)}, u32[]{:S(2)}) copy-start(f32[16,512]{1,0:T(8,128)} %param.49) | copy-start | bytes 98308
  354.5 205.5 %copy-start.33 = (f32[16,1536]{1,0:T(8,128)S(1)}, f32[16,1536]{1,0:T(8,128)}, u32[]{:S(2)}) copy-start(f32[16,1536]{1,0:T(8,128)} %param.48) | copy-start | bytes 294916
  354.5 347.8 %copy-start.30 = (f32[16,2048]{1,0:T(8,128)S(1)}, f32[16,2048]{1,0:T(8,128)}, u32[]{:S(2)}) copy-start(f32[16,2048]{1,0:T(8,128)} %param.50) | copy-start | bytes 393220
  354.5 487.1 %copy-start.31 = (f32[64,512]{1,0:T(8,128)S(1)}, f32[64,512]{1,0:T(8,128)}, u32[]{:S(2)}) copy-start(f32[64,512]{1,0:T(8,128)} %param.51) | copy-start | bytes 393220
  354.5 489.5 %copy-start.78 = (bf16[512,1536]{1,0:T(8,128)(2,1)S(1)}, bf16[512,1536]{1,0:T(8,128)(2,1)}, u32[]{:S(2)}) copy-start(bf16[512,1536]{1,0:T(8,128)(2,1)} %all-gather.8.cloned.1.call-done) | copy-start | bytes 4718596
  354.5 540.5 %all-gather.16.cloned.1.call-start = ((), (), s32[]{:S(2)}) async-start(), calls=%async_computation.11 | async-start | bytes 1081344 | tf_op jit(solution)/shard_map/all_gather | solution.py:248
  457.2 499.6 %all-gather.14.cloned.1.call-start = ((), (), s32[]{:S(2)}) async-start(), calls=%async_computation.9 | async-start | bytes 3244032 | tf_op jit(solution)/shard_map/all_gather | solution.py:248
  561.6 472.9 %all-gather.18.cloned.1.call-start = ((), (), s32[]{:S(2)}) async-start(), calls=%async_computation.13 | async-start | bytes 4325376 | tf_op jit(solution)/shard_map/all_gather | solution.py:248
  704.0 381.9 %all-gather.20.cloned.1.call-start = ((), (), s32[]{:S(2)}) async-start(), calls=%async_computation.15 | async-start | bytes 4325376 | tf_op jit(solution)/shard_map/all_gather | solution.py:248
  1104.1 111.3 %copy-start.4 = (bf16[8,196,512]{2,0,1:T(8,128)(2,1)S(1)}, bf16[8,196,512]{2,0,1:T(8,128)(2,1)}, u32[]{:S(2)}) copy-start(bf16[8,196,512]{2,0,1:T(8,128)(2,1)} %param.34) | copy-start | bytes 4816900
  1104.1 111.3 %copy-start.26 = (f32[8,196]{1,0:T(8,128)S(1)}, f32[8,196]{1,0:T(8,128)}, u32[]{:S(2)}) copy-start(f32[8,196]{1,0:T(8,128)} %copy-done.25) | copy-start | bytes 18820
  1104.2 111.3 %copy-start.41 = (f32[1,512]{1,0:T(1,128)S(1)}, f32[1,512]{1,0:T(1,128)}, u32[]{:S(2)}) copy-start(f32[1,512]{1,0:T(1,128)} %copy-done.40) | copy-start | bytes 6148
  1108.8 111.4 %copy-start.37 = (f32[8,196]{1,0:T(8,128)S(1)}, f32[8,196]{1,0:T(8,128)}, u32[]{:S(2)}) copy-start(f32[8,196]{1,0:T(8,128)} %copy-done.36) | copy-start | bytes 18820
  1108.8 111.4 %copy-start.29 = (f32[8,196]{1,0:T(8,128)S(1)}, f32[8,196]{1,0:T(8,128)}, u32[]{:S(2)}) copy-start(f32[8,196]{1,0:T(8,128)} %copy-done.28) | copy-start | bytes 18820
  1108.8 178.2 %all-to-all-start = ((bf16[32,2,16384]{2,1,0:T(2,128)(2,1)}), bf16[32,2,16384]{2,1,0:T(2,128)(2,1)}, u32[]{:S(2)}, u32[]{:S(2)}) async-start(bf16[32,2,16384]{2,1,0:T(2,128)(2,1)} %reshape.321), calls=%async_computation.4 | async-start | bytes 4194304 | tf_op jit(solution)/shard_map/all_to_all | solution.py:262
  1231.4 53.5 %copy-start.52 = (f32[2,512]{1,0:T(2,128)S(1)}, f32[2,512]{1,0:T(2,128)}, u32[]{:S(2)}) copy-start(f32[2,512]{1,0:T(2,128)} %param.45) | copy-start | bytes 12292
  1231.4 53.5 %copy-start.53 = (f32[2,512]{1,0:T(2,128)S(1)}, f32[2,512]{1,0:T(2,128)}, u32[]{:S(2)}) copy-start(f32[2,512]{1,0:T(2,128)} %param.44) | copy-start | bytes 12292
  1231.4 53.5 %copy-start.67 = (f32[2,512]{1,0:T(2,128)S(1)}, f32[2,512]{1,0:T(2,128)}, u32[]{:S(2)}) copy-start(f32[2,512]{1,0:T(2,128)} %param.55) | copy-start | bytes 12292
  1231.4 53.5 %copy-start.68 = (f32[2,512]{1,0:T(2,128)S(1)}, f32[2,512]{1,0:T(2,128)}, u32[]{:S(2)}) copy-start(f32[2,512]{1,0:T(2,128)} %param.54) | copy-start | bytes 12292
  1231.5 54.2 %copy-start.55 = (f32[169,16]{0,1:T(8,128)S(1)}, f32[169,16]{0,1:T(8,128)}, u32[]{:S(2)}) copy-start(f32[169,16]{0,1:T(8,128)} %param.47) | copy-start | bytes 32452
  1231.5 54.2 %copy-start.56 = (f32[169,16]{0,1:T(8,128)S(1)}, f32[169,16]{0,1:T(8,128)}, u32[]{:S(2)}) copy-start(f32[169,16]{0,1:T(8,128)} %param.59) | copy-start | bytes 32452
  1231.5 54.2 %copy-start.57 = (f32[169,16]{0,1:T(8,128)S(1)}, f32[169,16]{0,1:T(8,128)}, u32[]{:S(2)}) copy-start(f32[169,16]{0,1:T(8,128)} %param.58) | copy-start | bytes 32452
  (59 other events, 579.2 us)
Sparse Core Ops, SparseCore 0:
  10.9 58.5 all-gather.7
  72.3 55.4 all-gather.9
  130.6 55.2 all-gather.11
  322.1 133.6 reduce-scatter.6
  462.5 97.4 reduce-scatter.4
  562.2 140.0 reduce-scatter.8
  704.7 136.8 reduce-scatter.10
  845.5 49.5 all-gather.15
  898.9 57.8 all-gather.13
  960.5 60.8 all-gather.17
  1025.2 60.5 all-gather.19
where the time goes:
time: 1330 us; the launch traced here: 1320 us
  waiting for transfers between devices  609 us (46%)
  matrix products  214 us (16%)
  local copies, waits for them, and re-layouts  135 us (10%)
  other arithmetic  120 us (9%)
  starting transfers between devices  107 us (8%)
  blocking collectives  94.8 us (7%)
  loops' own time  25.9 us (2%)
  between operations  16.6 us (1%)
    reduce_scatter x1, waiting for transfers between devices, local(): lax.psum_scatter(expand_term, 'dp', scatter_dimension=0, tiled=True)  141 us
    reduce_scatter x1, waiting for transfers between devices, local(): lax.psum_scatter(project_term, 'dp', scatter_dimension=0, tiled=True)  137 us
    all_gather x4, waiting for transfers between devices, local(): whole = lax.all_gather(momenta_next, 'dp', axis=0, tiled=True)  121 us
    all_to_all x1, starting transfers between devices, local(): lax.all_to_all(as_sent(packed), 'dp', split_axis=0, concat_axis=0, tiled=...  107 us
    reduce_scatter x1, waiting for transfers between devices, local(): lax.psum_scatter(attend_term, 'dp', scatter_dimension=0, tiled=True)  103 us
    reduce_scatter x1, waiting for transfers between devices, local(): lax.psum_scatter(merge_term, 'dp', scatter_dimension=0, tiled=True)  101 us
    all_gather x1, blocking collectives, local(): lax.all_gather(merge_weight, 'dp', axis=0, tiled=True)  47.9 us
    psum x1, blocking collectives, local(): lax.psum((jnp.stack([gain_one, gain_two]), jnp.stack([shift_one, shift_tw...  46.8 us
  transfers between devices with their start and end apart: 12, of which 8 were waited for; matrix products, arithmetic and copies ran while one was open for 21% of the time, Pallas kernels for 0%

commit v1 on v0

--- a/solution.py
+++ b/solution.py
@@ -1,9 +1,10 @@
-from functools import partial
 import math
 
 import jax
 import jax.numpy as jnp
 from jax import lax
+from jax.experimental import pallas as pl
+from jax.experimental.pallas import tpu as pltpu
 from jax.sharding import PartitionSpec as P
 
 HEADS = 16
@@ -21,12 +22,191 @@
 newton_third = 2.0315
 
 
-def as_sent(shard):
-
-    def short(part):
-        return part.astype(jnp.bfloat16) if part.dtype == jnp.float32 else part
-
-    return jax.tree.map(short, shard)
+LANE = 512
+CELL = 8
+
+
+def device_bits(devices):
+    return devices.bit_length() - 1
+
+
+def swap(payload, devices, bit):
+    return lax.ppermute(payload, "dp", [(i, i ^ (1 << bit)) for i in range(devices)])
+
+
+def my_bit(rank, bit):
+    return (rank >> bit) & 1
+
+
+def gather_rows(pieces, rank, devices):
+    bits = device_bits(devices)
+    k, rows, lanes = pieces.shape
+    current = pieces.reshape((k,) + (1,) * bits + (rows, lanes))
+    for bit in list(range(3, bits)) + [2, 1, 0]:
+        axis = bits - bit
+        other = swap(current, devices, bit)
+        high = my_bit(rank, bit) == 1
+        current = jnp.concatenate(
+            [jnp.where(high, other, current), jnp.where(high, current, other)], axis=axis
+        )
+    return current.reshape(k, devices * rows, lanes)
+
+
+def split_wide(values):
+    high = lax.reduce_precision(values, 8, 7)
+    return high.astype(jnp.bfloat16), (values - high).astype(jnp.bfloat16)
+
+
+def reduce_rows(parts, wide, rank, devices):
+    bits = device_bits(devices)
+    planes = devices // CELL
+    running = []
+    for part in parts:
+        blocks, _, rows, lanes = part.shape
+        running.append(part.reshape(blocks, planes, 2, 2, 2, rows, lanes))
+
+    def encode(values):
+        sent = []
+        for value, keep in zip(values, wide):
+            for piece in split_wide(value) if keep else (value.astype(jnp.bfloat16),):
+                flat = jnp.moveaxis(piece, 0, -3)
+                sent.append(flat.reshape(flat.shape[:-3] + (-1, flat.shape[-1])))
+        return jnp.concatenate(sent, axis=-2)
+
+    def decode(payload, values):
+        out, start = [], 0
+        for value, keep in zip(values, wide):
+            blocks, rows = value.shape[0], value.shape[-2]
+            total = None
+            for _ in range(2 if keep else 1):
+                piece = payload[..., start : start + blocks * rows, :].astype(jnp.float32)
+                start += blocks * rows
+                piece = piece.reshape(piece.shape[:-2] + (blocks, rows, piece.shape[-1]))
+                piece = jnp.moveaxis(piece, -3, 0)
+                total = piece if total is None else total + piece
+            out.append(total)
+        return out
+
+    for bit, axis in ((0, 4), (1, 3), (2, 2)):
+        mine = my_bit(rank, bit)
+        give = [lax.dynamic_index_in_dim(r, 1 - mine, axis, keepdims=False) for r in running]
+        keep = [lax.dynamic_index_in_dim(r, mine, axis, keepdims=False) for r in running]
+        got = decode(swap(encode(give), devices, bit), give)
+        running = [k + g for k, g in zip(keep, got)]
+    plane = rank // CELL
+    total = [lax.dynamic_index_in_dim(r, plane, 1, keepdims=False) for r in running]
+    for step in range(1, planes):
+        target = (plane + step) % planes
+        give = [lax.dynamic_index_in_dim(r, target, 1, keepdims=False) for r in running]
+        pairs = [(i, (i + step * CELL) % devices) for i in range(devices)]
+        got = decode(lax.ppermute(encode(give), "dp", pairs), give)
+        total = [t + g for t, g in zip(total, got)]
+    return total
+
+
+def collect(rows, owners, rank, devices):
+    planes = devices // CELL
+    plane = rank // CELL
+    stacked = jnp.stack(rows)
+    pieces = [lax.dynamic_index_in_dim(stacked, jnp.clip(plane - owners[0], 0, len(owners) - 1), 0, keepdims=False)]
+    for step in range(1, planes):
+        target = (plane + step) % planes
+        give = lax.dynamic_index_in_dim(stacked, jnp.clip(target - owners[0], 0, len(owners) - 1), 0, keepdims=False)
+        pairs = [
+            (i, (i + step * CELL) % devices)
+            for i in range(devices)
+            if ((i // CELL + step) % planes) in owners
+        ]
+        pieces.append(lax.ppermute(give, "dp", pairs))
+    current = jnp.stack(pieces)[None]
+    for bit in (2, 1, 0):
+        pairs = [(i, i ^ (1 << bit)) for i in range(devices) if i // CELL in owners]
+        current = jnp.concatenate([current, lax.ppermute(current, "dp", pairs)], axis=0)
+    return current
+
+
+def split_bf16(values):
+    high = values.astype(jnp.bfloat16)
+    return high, (values - high.astype(jnp.float32)).astype(jnp.bfloat16)
+
+
+def dot_three(left, right, dims):
+    left_high, left_low = split_bf16(left)
+    right_high, right_low = split_bf16(right)
+
+    def one(a, b):
+        return lax.dot_general(a, b, (dims, ((), ())), preferred_element_type=jnp.float32)
+
+    return one(left_high, right_high) + (one(left_low, right_high) + one(left_high, right_low))
+
+
+PLAIN = ((1,), (0,))
+
+
+def newton_kernel(tall_ref, stack_ref, out_ref, gram_ref, poly_ref, total_ref):
+    tall = tall_ref[0] == 1
+    blocks = stack_ref.shape[0]
+    side = gram_ref.shape[0]
+    chunk = out_ref.shape[1]
+
+    @pl.when(tall)
+    def _():
+        total = jnp.zeros((side, side), jnp.float32)
+        for block in range(blocks):
+            values = stack_ref[block]
+            total = total + dot_three(values, values, ((0,), (0,)))
+        gram_ref[...] = total
+
+    @pl.when(jnp.logical_not(tall))
+    def _():
+        total = jnp.zeros((side, side), jnp.float32)
+        for block in range(blocks):
+            values = stack_ref[block]
+            total = total + dot_three(values, values, ((1,), (1,)))
+        gram_ref[...] = total
+
+    gram = gram_ref[...]
+    row = lax.broadcasted_iota(jnp.int32, (side, side), 0)
+    column = lax.broadcasted_iota(jnp.int32, (side, side), 1)
+    eye = (row == column).astype(jnp.float32)
+    norm = jnp.sqrt(jnp.sum(gram * eye)) + 1e-07
+    inverse = 1.0 / norm
+    gram_ref[...] = gram * (inverse * inverse)
+    poly_ref[...] = eye * inverse
+
+    def sweep(step, carry):
+        gram = gram_ref[...]
+        mixer = newton_first * eye + newton_second * gram + newton_third * dot_three(gram, gram, PLAIN)
+        poly_ref[...] = dot_three(poly_ref[...], mixer, PLAIN)
+        gram_ref[...] = dot_three(dot_three(gram, mixer, PLAIN), mixer, PLAIN)
+        return carry
+
+    lax.fori_loop(0, 5, sweep, 0)
+
+    @pl.when(tall)
+    def _():
+        for block in range(blocks):
+            out_ref[block] = dot_three(stack_ref[block, :chunk], poly_ref[...], PLAIN).astype(out_ref.dtype)
+
+    @pl.when(jnp.logical_not(tall))
+    def _():
+        for block in range(blocks):
+            out_ref[block] = dot_three(poly_ref[:chunk], stack_ref[block], PLAIN).astype(out_ref.dtype)
+
+
+def newton_rows(stack, tall, chunk):
+    blocks, side, lanes = stack.shape
+    return pl.pallas_call(
+        newton_kernel,
+        out_shape=jax.ShapeDtypeStruct((blocks, chunk, lanes), jnp.bfloat16),
+        in_specs=[
+            pl.BlockSpec(memory_space=pltpu.SMEM),
+            pl.BlockSpec(memory_space=pltpu.VMEM),
+        ],
+        out_specs=pl.BlockSpec(memory_space=pltpu.VMEM),
+        scratch_shapes=[pltpu.VMEM((side, side), jnp.float32)] * 3,
+        compiler_params=pltpu.CompilerParams(vmem_limit_bytes=48 << 20),
+    )(tall, stack)
 
 
 def layer_norm(values, gain, shift):
@@ -65,17 +245,6 @@
     return rows.transpose(0, 2, 1, 3).reshape(rows.shape[0], rows.shape[2], -1)
 
 
-def orthogonalize(matrix):
-    tall = matrix.shape[0] > matrix.shape[1]
-    current = matrix.T if tall else matrix
-    current = current / (jnp.sqrt(jnp.sum(current * current)) + 1e-07)
-    for sweep in range(5):
-        square = jnp.dot(current, current.T, precision=highest)
-        mixer = newton_second * square + newton_third * jnp.dot(square, square, precision=highest)
-        current = newton_first * current + jnp.dot(mixer, current, precision=highest)
-    return current.T if tall else current
-
-
 def adamw_step(param, grad, first, second, steps):
     first_next = 0.9 * first + 0.1 * grad
     second_next = 0.999 * second + 0.001 * grad * grad
@@ -85,8 +254,25 @@
     return (first_next, second_next, update)
 
 
-def padded_rows(flat, length):
-    return jnp.pad(flat, ((0, 0), (0, length - flat.shape[1])))
+def column_blocks(matrix):
+    rows, columns = matrix.shape
+    return jnp.transpose(matrix.reshape(rows, columns // LANE, LANE), (1, 0, 2))
+
+
+def from_blocks(blocks):
+    count, rows, lanes = blocks.shape
+    return jnp.transpose(blocks, (1, 0, 2)).reshape(rows, count * lanes)
+
+
+def by_owner(term, devices):
+    blocks = column_blocks(term)
+    return blocks.reshape(blocks.shape[0], devices, -1, LANE)
+
+
+def owner_form(moment, largest):
+    flat = column_blocks(moment).reshape(-1, LANE)
+    rows = largest - flat.shape[0]
+    return jnp.pad(flat, ((0, rows), (0, 0))).reshape(4, -1, LANE)
 
 
 def local(
@@ -125,13 +311,14 @@
     hidden_units = expand_weight.shape[1]
     scale = 1.0 / math.sqrt(width // HEADS)
     grad_scale = 1.0 / math.sqrt(slots * devices * PATCHES)
-    gathered = (
-        lax.all_gather(attend_weight, "dp", axis=0, tiled=True),
-        lax.all_gather(merge_weight, "dp", axis=0, tiled=True),
-        lax.all_gather(expand_weight, "dp", axis=0, tiled=True),
-        lax.all_gather(project_weight, "dp", axis=0, tiled=True),
-    )
-    attend_full, merge_full, expand_full, project_full = gathered
+    rank = lax.axis_index("dp")
+    planes = devices // CELL
+    first = jnp.concatenate([column_blocks(attend_weight), column_blocks(merge_weight)])
+    first_full = gather_rows(first, rank, devices)
+    attend_full = from_blocks(first_full[:3])
+    merge_full = first_full[3]
+    expand_full = from_blocks(gather_rows(column_blocks(expand_weight), rank, devices))
+    project_full = gather_rows(project_weight[None], rank, devices)[0]
     valid = (jnp.arange(slots) < image_counts[0]).astype(f32)[:, None, None]
     mask_add = -100.0 * (1 - shift_mask).astype(f32)
     masking = jnp.tile(mask_add, (slots, 1, 1))[:, None]
@@ -175,12 +362,7 @@
         + layer_biases[4 * width + hidden_units :]
     )
     block_out = (valid * (middle + mlp_out)).astype(bf16)
-    attend_back, merge_back, expand_back, project_back = (
-        lax.all_gather(attend_weight, "dp", axis=0, tiled=True),
-        lax.all_gather(merge_weight, "dp", axis=0, tiled=True),
-        lax.all_gather(expand_weight, "dp", axis=0, tiled=True),
-        lax.all_gather(project_weight, "dp", axis=0, tiled=True),
-    )
+    attend_back, merge_back, expand_back, project_back = (attend_full, merge_full, expand_full, project_full)
     grad_out = valid * cotangent.astype(f32)
     grad_out_low = grad_out.astype(bf16)
     project_term = jnp.einsum("itf,itd->fd", active_low, grad_out_low, preferred_element_type=f32)
@@ -226,12 +408,14 @@
             jnp.sum(grad_out_low, axis=(0, 1), dtype=f32),
         ]
     )
-    mat_sums = (
-        lax.psum_scatter(attend_term, "dp", scatter_dimension=0, tiled=True),
-        lax.psum_scatter(merge_term, "dp", scatter_dimension=0, tiled=True),
-        lax.psum_scatter(expand_term, "dp", scatter_dimension=0, tiled=True),
-        lax.psum_scatter(project_term, "dp", scatter_dimension=0, tiled=True),
-    )
+    merge_sum, expand_sum, project_sum = reduce_rows(
+        [by_owner(merge_term, devices), by_owner(expand_term, devices), by_owner(project_term, devices)],
+        (True, False, False),
+        rank,
+        devices,
+    )
+    (attend_sum,) = reduce_rows([by_owner(attend_term, devices)], (False,), rank, devices)
+    mat_sums = tuple(from_blocks(term) for term in (attend_sum, merge_sum, expand_sum, project_sum))
     small_sums = lax.psum(
         (jnp.stack([gain_one, gain_two]), jnp.stack([shift_one, shift_two]), bias_term, table_term),
         "dp",
@@ -240,37 +424,34 @@
     small_grads = tuple((term * grad_scale for term in small_sums))
     momenta = (attend_momentum, merge_momentum, expand_momentum, project_momentum)
     momenta_next = tuple((0.95 * moment + grad for moment, grad in zip(momenta, mat_grads)))
-    stride = 1
-    owner_ranks = [order * stride for order in range(4)]
-    rank_index = lax.axis_index("dp")
-    shard_sizes = [moment.size for moment in momenta_next]
-    longest = max(shard_sizes)
-    whole = lax.all_gather(momenta_next, "dp", axis=0, tiled=True)
-    owner_terms = tuple(
-        (
-            lax.cond(
-                rank_index == owner_ranks[order],
-                partial(orthogonalize, matrix),
-                partial(jnp.zeros_like, matrix),
-            )
-            for order, matrix in enumerate(whole)
-        )
-    )
-    packed = jnp.zeros((devices, longest), f32)
-    for order, term in enumerate(owner_terms):
-        packed = packed + padded_rows(term.reshape(devices, shard_sizes[order]), longest)
-    received = lax.all_to_all(
-        as_sent(packed), "dp", split_axis=0, concat_axis=0, tiled=True
-    ).astype(packed.dtype)
-    orth_rows = tuple(
-        (
-            received[owner_ranks[order], : shard_sizes[order]].reshape(moment.shape)
-            for order, moment in enumerate(momenta_next)
-        )
-    )
+    largest = project_momentum.shape[0]
+    packed = [owner_form(moment, largest) for moment in momenta_next]
+    rest = collect(packed[1:], (1, 2, 3), rank, devices)
+    head = collect(packed[:1], (0,), rank, devices)
+    plane = rank // CELL
+    whole = jnp.where(plane == 0, head, rest)
+    stack = jnp.transpose(whole, (2, 0, 1, 3, 4)).reshape(4, -1, LANE)
+    tall = (plane == 3).astype(jnp.int32).reshape(1)
+    chunk = planes * packed[0].shape[1]
+    orth = newton_rows(stack, tall, chunk).reshape(4, planes, -1, LANE)
+    pieces = []
+    for step in range(planes):
+        give = orth[:, (planes - step) % planes]
+        if step:
+            pairs = [(i, (i + step * CELL) % devices) for i in range(devices) if i // CELL < 4]
+            give = lax.ppermute(give, "dp", pairs)
+        pieces.append(give)
+    received = jnp.stack(pieces)
+    orth_rows = []
+    for order, moment in enumerate(momenta_next):
+        piece = lax.dynamic_index_in_dim(received, (plane - order) % planes, 0, keepdims=False)
+        blocks, rows = max(moment.shape[1] // LANE, 1), moment.shape[0]
+        piece = piece.reshape(-1, LANE)[: blocks * rows].reshape(blocks, rows, LANE)
+        orth_rows.append(from_blocks(piece).astype(f32))
     results = [block_out, input_grad]
-    for grad, moment_next, orth_part, matrix in zip(mat_grads, momenta_next, orth_rows, whole):
-        update = -0.02 * math.sqrt(max(matrix.shape)) * orth_part
+    for grad, moment_next, orth_part in zip(mat_grads, momenta_next, orth_rows):
+        extent = max(devices * moment_next.shape[0], moment_next.shape[1])
+        update = -0.02 * math.sqrt(extent) * orth_part
         results += [grad, moment_next, update]
     steps = step_count[0].astype(f32)
     params = (norm_gains, norm_shifts, layer_biases, bias_table)

time: 1330 us -> 744 us (0.56)
  waiting for transfers between devices: 609 us -> 74.2 us
  local copies, waits for them, and re-layouts: 135 us -> 229 us
  matrix products: 214 us -> 143 us
  starting transfers between devices: 107 us -> 63.4 us
  blocking collectives: 94.8 us -> 51.2 us
  loops' own time: 25.9 us -> 0 us
  Pallas kernels: 0 us -> 23.5 us
  other arithmetic: 120 us -> 142 us
    reduce_scatter x4 -> x0, waiting for transfers between devices: 482 us -> none  [the longest x1 141 us: local(): lax.psum_scatter(expand_term, 'dp', scatter_dimension=0, tiled=True)]
    all_gather x7 -> x0, waiting for transfers between devices: 125 us -> none  [the longest x4 121 us: local(): whole = lax.all_gather(momenta_next, 'dp', axis=0, tiled=True)]
    all_to_all x1 -> x0, starting transfers between devices: 107 us -> none  [local(): lax.all_to_all(as_sent(packed), 'dp', split_axis=0, concat_axis=0, tiled=...]
    ppermute x0 -> x42, waiting for transfers between devices: none -> 74.2 us  [the longest x21 63.1 us: swap(): lax.ppermute(payload, 'dp', [(i, i ^ 1 << bit) for i in range(devices)])]
    dot_general x15 -> x0, matrix products: 67.2 us -> none  [the longest x5 30.2 us: orthogonalize(): square = jnp.dot(current, current.T, precision=highest)]
    ppermute x0 -> x42, starting transfers between devices: none -> 63.4 us  [the longest x21 24.2 us: swap(): lax.ppermute(payload, 'dp', [(i, i ^ 1 << bit) for i in range(devices)])]
    all_gather x1 -> x0, blocking collectives: 47.9 us -> none  [local(): lax.all_gather(merge_weight, 'dp', axis=0, tiled=True)]
    another operation x0 -> x5, local copies, waits for them, and re-layouts: none -> 37.5 us
  transfers between devices with their start and end apart: 12 -> 42, of which waited for: 8 -> 13; matrix products, arithmetic and copies ran while one was open for 21% -> 37% of each run, Pallas kernels for 0% -> 0%
where the time goes in v1:
time: 744 us; the launch traced here: 731 us
  local copies, waits for them, and re-layouts  229 us (31%)
  matrix products  143 us (19%)
  other arithmetic  142 us (19%)
  waiting for transfers between devices  74.2 us (10%)
  starting transfers between devices  63.4 us (9%)
  blocking collectives  51.2 us (7%)
  Pallas kernels  23.5 us (3%)
    ppermute x21, waiting for transfers between devices, swap(): lax.ppermute(payload, 'dp', [(i, i ^ 1 << bit) for i in range(devices)])  63.1 us
    psum x1, blocking collectives, local(): lax.psum((jnp.stack([gain_one, gain_two]), jnp.stack([shift_one, shift_tw...  51.2 us
    another operation x3, local copies, waits for them, and re-layouts  36.7 us
    convert_element_type x1, other arithmetic, local(): active_low = activated.astype(bf16)  31.6 us
    mul x4, local copies, waits for them, and re-layouts, local(): merge_heads(grad_queries) * scale  30.9 us
    concatenate x4, local copies, waits for them, and re-layouts, local(): jnp.concatenate([merge_heads(grad_queries) * scale, merge_heads(grad_keys...  24.5 us
    ppermute x21, starting transfers between devices, swap(): lax.ppermute(payload, 'dp', [(i, i ^ 1 << bit) for i in range(devices)])  24.2 us
    pallas_call x1, Pallas kernels, newton_rows(): pl.pallas_call(newton_kernel, out_shape=jax.ShapeDtypeStruct((blocks, chu...  23.5 us
  transfers between devices with their start and end apart: 42, of which 13 were waited for; matrix products, arithmetic and copies ran while one was open for 37% of the time, Pallas kernels for 0%

profile of v1, /device:TPU:0, one launch (start us, length us, event | category | flops | bytes accessed | tf_op | source)
XLA Modules:
  0.0 731.2 jit_solution(2898719692955135182)
XLA Ops:
  29.4 7.0 collective-permute-done.11
  43.7 7.7 %collective-permute-done.2 = bf16[4,2,2,1,1,1,16,512]{7,0,6,5,4,3,2,1:T(4,128)(2,1)S(1)} collective-permute-done((bf16[4,2,2,1,1,1,16,512]{7,0,6,5,4,3,2,1:T(4,128)(2,1)S(1)}, bf16[4,2,2,1,1,1,16,512]{7,0,6,5,4,3,2,1:T(4,128)(2,1)S(1)}, u32[]{:S(2)}, u32[]{:S(2)}) %collective-permute-start.2) | collective-permute-done | bytes 262176 | tf_op jit(solution)/shard_map/ppermute | solution.py:34
  58.6 8.3 %collective-permute-done.3 = bf16[4,2,2,2,1,1,16,512]{7,0,6,5,4,3,2,1:T(4,128)(2,1)S(1)} collective-permute-done((bf16[4,2,2,2,1,1,16,512]{7,0,6,5,4,3,2,1:T(4,128)(2,1)S(1)}, bf16[4,2,2,2,1,1,16,512]{7,0,6,5,4,3,2,1:T(4,128)(2,1)S(1)}, u32[]{:S(2)}, u32[]{:S(2)}) %collective-permute-start.3) | collective-permute-done | bytes 524320 | tf_op jit(solution)/shard_map/ppermute | solution.py:34
  98.0 8.4 %fusion.113 = (bf16[32,49,1536]{2,0,1:T(8,128)(2,1)S(1)}, f32[32,49,1536]{2,0,1:T(8,128)}) fusion(f32[1536]{0:T(1024)S(1)} %slice-done.2, bf16[32,49,512]{2,0,1:T(8,128)(2,1)} %reshape.635, bf16[512,1536,1]{0,1,2:T(8,128)(2,1)} %bitcast.460), kind=kOutput, calls=%fused_computation.321 | convolution fusion | flops 2471067648 | bytes 17635328 | tf_op jit(solution)/shard_map/wtd,de->wte/dot_general | solution.py:331
  127.2 11.9 %fusion.114 = (f32[32,16,49]{2,1,0:T(8,128)S(1)}, f32[32,16,49,49]{2,3,1,0:T(8,128)}) fusion(f32[32,49,49]{1,2,0:T(8,128)S(1)} %bitcast.464, f32[16,49,49]{1,2,0:T(8,128)} %copy.332, bf16[32,16,49,32]{2,3,1,0:T(8,128)(2,1)} %bitcast.424, bf16[32,16,49,32]{2,3,1,0:T(8,128)(2,1)} %bitcast.422), kind=kOutput, calls=%fused_computation.322 | convolution fusion | flops 83593264 | bytes 8689856 | tf_op jit(solution)/shard_map/sub | solution.py:342
  139.8 7.5 %fusion.41 = bf16[32,16,49,32]{2,3,1,0:T(8,128)(2,1)S(1)} fusion(bf16[32,16,49,32]{2,3,1,0:T(8,128)(2,1)} %bitcast.448, f32[32,16,49,49]{2,3,1,0:T(8,128)} %get-tuple-element.298, f32[32,16,49]{2,1,0:T(8,128)S(1)} %get-tuple-element.297), kind=kOutput, calls=%fused_computation.94 | convolution fusion | flops 81937408 | bytes 8228864 | tf_op jit(solution)/shard_map/whqk,whkc->whqc/dot_general | solution.py:345
  184.1 7.3 fusion.36
  191.4 31.6 %multiply_convert_fusion.1 = (bf16[8,196,2048]{2,1,0:T(8,128)(2,1)}, f32[8,196,2048]{2,1,0:T(8,128)}) fusion(f32[8,196,2048]{2,1,0:T(8,128)S(1)} %get-tuple-element.299, f32[2048]{0:T(1024)S(1)} %slice.217, u8[196,2048]{1,0:T(8,128)(4,1)S(1)} %get-tuple-element.181, u8[196,2048]{1,0:T(8,128)(4,1)S(1)} %get-tuple-element.180), kind=kLoop, calls=%fused_computation.15 | loop fusion | flops 227999744 | bytes 32923648 | tf_op jit(solution)/shard_map/convert_element_type | solution.py:359
  223.0 16.9 %convert_reduce_fusion.1 = (f32[2048]{0:T(1024)}, bf16[8,196,2048]{2,1,0:T(8,128)(2,1)S(1)}) fusion(f32[8,196,2048]{2,1,0:T(8,128)} %get-tuple-element.221, bf16[2048,512,1]{1,0,2:T(8,128)(2,1)} %bitcast.455, f32[8]{0:T(128)S(1)} %copy-done.117, bf16[8,196,512]{2,0,1:T(8,128)(2,1)} %param.27, f32[8,196,2048]{2,1,0:T(8,128)} %copy-done.12, f32[2048]{0:T(1024)S(1)} %slice.217), kind=kOutput, calls=%fused_computation.13 | convolution fusion | flops 3345332224 | bytes 35831840 | tf_op jit(solution)/shard_map/itd,fd->itf/dot_general | solution.py:369
  239.9 8.3 %fusion.102 = (f32[512]{0:T(512)}, f32[8,196]{1,0:T(8,128)S(1)}, f32[8,196,512]{2,1,0:T(8,128)S(1)}) fusion(f32[512]{0:T(512)S(1)} %bitcast.510, f32[8,196,512]{2,1,0:T(8,128)S(1)} %get-tuple-element.223, f32[8,196]{1,0:T(8,128)S(1)} %broadcast_multiply_fusion.2, bf16[8,196,2048]{2,1,0:T(8,128)(2,1)S(1)} %get-tuple-element.304, ...), kind=kOutput, calls=%fused_computation.313 | convolution fusion | flops 3292346368 | bytes 14958848 | tf_op jit(solution)/shard_map/itf,df->itd/dot_general | solution.py:372
  268.4 8.1 %reshape.647 = bf16[32,49,16,32]{3,2,0,1:T(8,128)(2,1)} reshape(bf16[32,49,512]{2,0,1:T(8,128)(2,1)} %copy.344) | data formatting | bytes 3211264 | tf_op jit(solution)/shard_map/reshape | solution.py:241
  276.5 10.5 %copy.345 = bf16[32,16,49,32]{2,3,1,0:T(8,128)(2,1)} copy(bf16[32,16,49,32]{3,1,0,2:T(8,128)(2,1)} %bitcast.417) | data formatting | bytes 3211264 | tf_op jit(solution)/shard_map/transpose | solution.py:241
  287.0 14.8 %multiply_reduce_fusion = (f32[32,16,49]{2,1,0:T(8,128)S(1)}, f32[32,16,49,49]{2,3,1,0:T(8,128)}) fusion(f32[32,16,49,49]{2,3,1,0:T(8,128)} %get-tuple-element.298, f32[32,16,49]{2,1,0:T(8,128)} %copy-done.72, bf16[32,16,49,32]{2,3,1,0:T(8,128)(2,1)} %copy.345, bf16[32,16,49,32]{2,3,1,0:T(8,128)(2,1)} %bitcast.449), kind=kOutput, calls=%fused_computation.4 | convolution fusion | flops 82338816 | bytes 13246464 | tf_op jit(solution)/shard_map/whqc,whkc->whqk/dot_general | solution.py:383
  301.8 14.6 %convert_reduce_fusion = (f32[16,49,49]{1,2,0:T(8,128)}, bf16[32,16,49,49]{2,3,1,0:T(8,128)(2,1)}) fusion(f32[32,16,49,49]{2,3,1,0:T(8,128)} %get-tuple-element.302, f32[32,16,49]{2,1,0:T(8,128)S(1)} %get-tuple-element.301, f32[32,16,49,49]{2,3,1,0:T(8,128)} %get-tuple-element.298, f32[32,16,49]{2,1,0:T(8,128)S(1)} %copy-done.73), kind=kLoop, calls=%fused_computation.2 | loop fusion | flops 7337456 | bytes 12647488 | tf_op jit(solution)/shard_map/reduce_sum | solution.py:389
  316.4 8.4 %multiply_convert_fusion.2 = bf16[32,16,49,32]{2,3,1,0:T(8,128)(2,1)} fusion(bf16[32,16,49,49]{2,3,1,0:T(8,128)(2,1)} %get-tuple-element.209, bf16[32,16,49,32]{2,3,1,0:T(8,128)(2,1)} %bitcast.423), kind=kOutput, calls=%fused_computation.30 | convolution fusion | flops 80281600 | bytes 5669888 | tf_op jit(solution)/shard_map/whqk,whkc->whqc/dot_general | solution.py:391
  324.8 10.3 %convolution_convert_fusion = bf16[32,16,49,32]{2,3,1,0:T(8,128)(2,1)} fusion(bf16[32,16,49,49]{2,3,1,0:T(8,128)(2,1)} %get-tuple-element.209, bf16[32,16,49,32]{2,3,1,0:T(8,128)(2,1)} %bitcast.425), kind=kOutput, calls=%fused_computation.96 | convolution fusion | flops 79478784 | bytes 5669888 | tf_op jit(solution)/shard_map/whqk,whqc->whkc/dot_general | solution.py:392
  335.1 9.9 %fusion.44 = bf16[32,16,49,32]{2,3,1,0:T(8,128)(2,1)} fusion(bf16[32,16,49,32]{2,3,1,0:T(8,128)(2,1)} %copy.345, f32[32,16,49,49]{2,3,1,0:T(8,128)} %get-tuple-element.298, f32[32,16,49]{2,1,0:T(8,128)S(1)} %copy-done.74), kind=kOutput, calls=%fused_computation.95 | convolution fusion | flops 81937408 | bytes 8228864 | tf_op jit(solution)/shard_map/whqk,whqc->whkc/dot_general | solution.py:380
  382.0 11.4 %copy.375 = bf16[4,2,2,2,16,49,32]{6,4,5,3,2,1,0:T(8,128)(2,1)} copy(bf16[4,2,2,2,16,49,32]{5,4,3,2,1,0,6:T(8,128)(2,1)} %bitcast.419) | data formatting | bytes 3211264 | tf_op jit(solution)/shard_map/reshape.336
  399.2 7.1 fusion.99
  419.4 12.5 %copy.347 = bf16[32,49,16,32]{3,2,0,1:T(8,128)(2,1)} copy(bf16[32,49,16,32]{1,3,2,0:T(8,128)(2,1)} %bitcast.416) | data formatting | bytes 3211264 | tf_op jit(solution)/shard_map/mul | solution.py:394
  431.9 9.9 %mul.469 = bf16[8,2,2,7,7,512]{5,2,1,0,4,3:T(2,128)(2,1)} reshape(bf16[32,49,16,32]{3,2,0,1:T(8,128)(2,1)} %copy.347) | data formatting | bytes 3211264 | tf_op jit(solution)/shard_map/mul | solution.py:394
  444.7 12.7 %copy.349 = bf16[32,49,16,32]{3,2,0,1:T(8,128)(2,1)} copy(bf16[32,49,16,32]{1,3,2,0:T(8,128)(2,1)} %bitcast.414) | data formatting | bytes 3211264 | tf_op jit(solution)/shard_map/convert.30
  457.4 9.9 %concatenate.155 = bf16[8,2,2,7,7,512]{5,2,1,0,4,3:T(2,128)(2,1)} reshape(bf16[32,49,16,32]{3,2,0,1:T(8,128)(2,1)} %copy.349) | data formatting | bytes 3211264 | tf_op jit(solution)/shard_map/concatenate | solution.py:393
  470.2 12.6 %copy.352 = bf16[32,49,16,32]{3,2,0,1:T(8,128)(2,1)} copy(bf16[32,49,16,32]{1,3,2,0:T(8,128)(2,1)} %bitcast.421) | data formatting | bytes 3211264 | tf_op jit(solution)/shard_map/convert.29
  482.8 9.9 %concatenate.156 = bf16[8,2,2,7,7,512]{5,2,1,0,4,3:T(2,128)(2,1)} reshape(bf16[32,49,16,32]{3,2,0,1:T(8,128)(2,1)} %copy.352) | data formatting | bytes 3211264 | tf_op jit(solution)/shard_map/concatenate | solution.py:393
  518.1 19.3 %collective-permute-done.28 = bf16[4,2,160,512]{3,2,1,0:T(8,128)(2,1)S(1)} collective-permute-done((bf16[4,2,160,512]{3,2,1,0:T(8,128)(2,1)S(1)}, bf16[4,2,160,512]{3,2,1,0:T(8,128)(2,1)S(1)}, u32[]{:S(2)}, u32[]{:S(2)}) %collective-permute-start.28) | collective-permute-done | bytes 1310752 | tf_op jit(solution)/shard_map/ppermute | solution.py:34
  545.7 8.3 %collective-permute-done.29 = bf16[4,160,512]{2,1,0:T(8,128)(2,1)S(1)} collective-permute-done((bf16[4,160,512]{2,1,0:T(8,128)(2,1)S(1)}, bf16[4,160,512]{2,1,0:T(8,128)(2,1)S(1)}, u32[]{:S(2)}, u32[]{:S(2)}) %collective-permute-start.29) | collective-permute-done | bytes 655392 | tf_op jit(solution)/shard_map/ppermute | solution.py:34
  580.8 7.4 %collective-permute-start.33 = (f32[4,16,512]{2,1,0:T(8,128)S(1)}, f32[4,16,512]{2,1,0:T(8,128)S(1)}, u32[]{:S(2)}, u32[]{:S(2)}) collective-permute-start(f32[4,16,512]{2,1,0:T(8,128)S(1)} %get-tuple-element.259), channel_id=1, source_target_pairs={{0,8},{1,9},{2,10},{3,11},{4,12},{5,13},{6,14},{7,15},{8,16},{9,17... | collective-permute-start | bytes 393224 | tf_op jit(solution)/shard_map/ppermute | solution.py:120
  603.3 7.2 collective-permute-done.24
  622.5 51.2 %all-reduce.2 = (f32[2,512]{1,0:T(2,128)S(1)}, f32[2,512]{1,0:T(2,128)S(1)}, f32[4608]{0:T(1024)S(1)}, f32[169,16]{0,1:T(8,128)S(1)}) all-reduce(f32[2,512]{1,0:T(2,128)S(1)} %pad_maximum_fusion.36, f32[2,512]{1,0:T(2,128)S(1)} %pad_maximum_fusion.37, f32[4608]{0:T(1024)S(1)} %pad_maximum_fusion.35, ...), channel_id=1, replica_groups=mesh['dp'=32] {'dp'}, use_global_device_ids=true, to_apply=%region_13.14 | all-reduce | flops 9360 | bytes 74880 | tf_op jit(solution)/shard_map/psum | solution.py:419
  685.9 6.7 multiply_convert_fusion.3
  694.9 23.5 %shard_map.481 = bf16[4,64,512]{2,1,0:T(8,128)(2,1)S(1)} custom-call(s32[1]{0:T(128)} %bitcast.89.tall_ref, f32[4,512,512]{2,1,0:T(8,128)S(1)} %bitcast.408), custom_call_target="tpu_custom_call" | custom-call | tf_op jit(solution)/shard_map/pallas_call | solution.py:199
  (524 shorter events, 325.6 us)
Async XLA Ops:
  0.7 20.9 %collective-permute-start.10 = (bf16[1,1,1,1,1,1,64,512]{7,6,5,4,3,2,1,0:T(8,128)(2,1)}, bf16[1,1,1,1,1,1,64,512]{7,6,5,4,3,2,1,0:T(8,128)(2,1)}, u32[]{:S(2)}, u32[]{:S(2)}) collective-permute-start(bf16[1,1,1,1,1,1,64,512]{7,6,5,4,3,2,1,0:T(8,128)(2,1)} %bitcast.501), channel_id=1, source_target_pairs={{0,8},{1,9},{2,10},{3,11},{4,12},{5,13},{6,14},{7,15},{8,0},{9,1},... | collective-permute-start | bytes 196616 | tf_op jit(solution)/shard_map/ppermute | solution.py:34
  6.1 19.0 %collective-permute-start = (bf16[4,1,1,1,1,1,16,512]{7,0,6,5,4,3,2,1:T(4,128)(2,1)}, bf16[4,1,1,1,1,1,16,512]{7,0,6,5,4,3,2,1:T(4,128)(2,1)}, u32[]{:S(2)}, u32[]{:S(2)}) collective-permute-start(bf16[4,1,1,1,1,1,16,512]{7,0,6,5,4,3,2,1:T(4,128)(2,1)} %maximum_bitcast_fusion.2), channel_id=1, source_target_pairs={{0,8},{1,9},{2,10},{3,11},{4,12},{5,13},{6,14},{7,15},{8,0},{9,1},... | collective-permute-start | bytes 196616 | tf_op jit(solution)/shard_map/ppermute | solution.py:34
  7.1 18.0 %collective-permute-start.5 = (bf16[4,1,1,1,1,1,16,512]{7,0,6,5,4,3,2,1:T(4,128)(2,1)S(1)}, bf16[4,1,1,1,1,1,16,512]{7,0,6,5,4,3,2,1:T(4,128)(2,1)}, u32[]{:S(2)}, u32[]{:S(2)}) collective-permute-start(bf16[4,1,1,1,1,1,16,512]{7,0,6,5,4,3,2,1:T(4,128)(2,1)S(1)} %bitcast.483), channel_id=1, source_target_pairs={{0,8},{1,9},{2,10},{3,11},{4,12},{5,13},{6,14},{7,15},{8,0},{9,1},... | collective-permute-start | bytes 196616 | tf_op jit(solution)/shard_map/ppermute | solution.py:34
  22.5 13.9 %collective-permute-start.11 = (bf16[1,1,2,1,1,1,64,512]{7,6,5,4,3,2,1,0:T(8,128)(2,1)S(1)}, bf16[1,1,2,1,1,1,64,512]{7,6,5,4,3,2,1,0:T(8,128)(2,1)S(1)}, u32[]{:S(2)}, u32[]{:S(2)}) collective-permute-start(bf16[1,1,2,1,1,1,64,512]{7,6,5,4,3,2,1,0:T(8,128)(2,1)S(1)} %pad_maximum_fusion.34), channel_id=1, source_target_pairs={{0,16},{1,17},{2,18},{3,19},{4,20},{5,21},{6,22},{7,23},{8,24},{9,... | collective-permute-start | bytes 393224 | tf_op jit(solution)/shard_map/ppermute | solution.py:34
  26.2 12.9 %collective-permute-start.1 = (bf16[4,1,2,1,1,1,16,512]{7,0,6,5,4,3,2,1:T(4,128)(2,1)S(1)}, bf16[4,1,2,1,1,1,16,512]{7,0,6,5,4,3,2,1:T(4,128)(2,1)S(1)}, u32[]{:S(2)}, u32[]{:S(2)}) collective-permute-start(bf16[4,1,2,1,1,1,16,512]{7,0,6,5,4,3,2,1:T(4,128)(2,1)S(1)} %pad_maximum_fusion.32), channel_id=1, source_target_pairs={{0,16},{1,17},{2,18},{3,19},{4,20},{5,21},{6,22},{7,23},{8,24},{9,... | collective-permute-start | bytes 393224 | tf_op jit(solution)/shard_map/ppermute | solution.py:34
  26.7 15.0 %collective-permute-start.6 = (bf16[4,1,2,1,1,1,16,512]{7,0,6,5,4,3,2,1:T(4,128)(2,1)S(1)}, bf16[4,1,2,1,1,1,16,512]{7,0,6,5,4,3,2,1:T(4,128)(2,1)S(1)}, u32[]{:S(2)}, u32[]{:S(2)}) collective-permute-start(bf16[4,1,2,1,1,1,16,512]{7,0,6,5,4,3,2,1:T(4,128)(2,1)S(1)} %pad_maximum_fusion.33), channel_id=1, source_target_pairs={{0,16},{1,17},{2,18},{3,19},{4,20},{5,21},{6,22},{7,23},{8,24},{9,... | collective-permute-start | bytes 393224 | tf_op jit(solution)/shard_map/ppermute | solution.py:34
  36.4 17.7 %collective-permute-start.12 = (bf16[1,2,2,1,1,1,64,512]{7,6,5,4,3,2,1,0:T(8,128)(2,1)S(1)}, bf16[1,2,2,1,1,1,64,512]{7,6,5,4,3,2,1,0:T(8,128)(2,1)S(1)}, u32[]{:S(2)}, u32[]{:S(2)}) collective-permute-start(bf16[1,2,2,1,1,1,64,512]{7,6,5,4,3,2,1,0:T(8,128)(2,1)S(1)} %pad_maximum_fusion.27), channel_id=1, source_target_pairs={{0,4},{1,5},{2,6},{3,7},{4,0},{5,1},{6,2},{7,3},{8,12},{9,13},{10,... | collective-permute-start | bytes 786440 | tf_op jit(solution)/shard_map/ppermute | solution.py:34
  39.5 11.8 %collective-permute-start.2 = (bf16[4,2,2,1,1,1,16,512]{7,0,6,5,4,3,2,1:T(4,128)(2,1)S(1)}, bf16[4,2,2,1,1,1,16,512]{7,0,6,5,4,3,2,1:T(4,128)(2,1)S(1)}, u32[]{:S(2)}, u32[]{:S(2)}) collective-permute-start(bf16[4,2,2,1,1,1,16,512]{7,0,6,5,4,3,2,1:T(4,128)(2,1)S(1)} %pad_maximum_fusion.25), channel_id=1, source_target_pairs={{0,4},{1,5},{2,6},{3,7},{4,0},{5,1},{6,2},{7,3},{8,12},{9,13},{10,... | collective-permute-start | bytes 786440 | tf_op jit(solution)/shard_map/ppermute | solution.py:34
  42.0 13.4 %collective-permute-start.7 = (bf16[4,2,2,1,1,1,16,512]{7,0,6,5,4,3,2,1:T(4,128)(2,1)S(1)}, bf16[4,2,2,1,1,1,16,512]{7,0,6,5,4,3,2,1:T(4,128)(2,1)S(1)}, u32[]{:S(2)}, u32[]{:S(2)}) collective-permute-start(bf16[4,2,2,1,1,1,16,512]{7,0,6,5,4,3,2,1:T(4,128)(2,1)S(1)} %pad_maximum_fusion.26), channel_id=1, source_target_pairs={{0,4},{1,5},{2,6},{3,7},{4,0},{5,1},{6,2},{7,3},{8,12},{9,13},{10,... | collective-permute-start | bytes 786440 | tf_op jit(solution)/shard_map/ppermute | solution.py:34
  52.0 14.9 %collective-permute-start.3 = (bf16[4,2,2,2,1,1,16,512]{7,0,6,5,4,3,2,1:T(4,128)(2,1)S(1)}, bf16[4,2,2,2,1,1,16,512]{7,0,6,5,4,3,2,1:T(4,128)(2,1)S(1)}, u32[]{:S(2)}, u32[]{:S(2)}) collective-permute-start(bf16[4,2,2,2,1,1,16,512]{7,0,6,5,4,3,2,1:T(4,128)(2,1)S(1)} %pad_maximum_fusion.21), channel_id=1, source_target_pairs={{0,2},{1,3},{2,0},{3,1},{4,6},{5,7},{6,4},{7,5},{8,10},{9,11},{10,... | collective-permute-start | bytes 1572872 | tf_op jit(solution)/shard_map/ppermute | solution.py:34
  55.1 23.2 %collective-permute-start.13 = (bf16[1,2,2,2,1,1,64,512]{7,6,5,4,3,2,1,0:T(8,128)(2,1)}, bf16[1,2,2,2,1,1,64,512]{7,6,5,4,3,2,1,0:T(8,128)(2,1)}, u32[]{:S(2)}, u32[]{:S(2)}) collective-permute-start(bf16[1,2,2,2,1,1,64,512]{7,6,5,4,3,2,1,0:T(8,128)(2,1)} %pad_maximum_fusion.23), channel_id=1, source_target_pairs={{0,2},{1,3},{2,0},{3,1},{4,6},{5,7},{6,4},{7,5},{8,10},{9,11},{10,... | collective-permute-start | bytes 1572872 | tf_op jit(solution)/shard_map/ppermute | solution.py:34
  57.0 28.6 %collective-permute-start.8 = (bf16[4,2,2,2,1,1,16,512]{7,0,6,5,4,3,2,1:T(4,128)(2,1)}, bf16[4,2,2,2,1,1,16,512]{7,0,6,5,4,3,2,1:T(4,128)(2,1)}, u32[]{:S(2)}, u32[]{:S(2)}) collective-permute-start(bf16[4,2,2,2,1,1,16,512]{7,0,6,5,4,3,2,1:T(4,128)(2,1)} %pad_maximum_fusion.22), channel_id=1, source_target_pairs={{0,2},{1,3},{2,0},{3,1},{4,6},{5,7},{6,4},{7,5},{8,10},{9,11},{10,... | collective-permute-start | bytes 1572872 | tf_op jit(solution)/shard_map/ppermute | solution.py:34
  69.2 19.8 %collective-permute-start.4 = (bf16[4,2,2,2,2,1,16,512]{7,0,6,5,4,3,2,1:T(4,128)(2,1)}, bf16[4,2,2,2,2,1,16,512]{7,0,6,5,4,3,2,1:T(4,128)(2,1)}, u32[]{:S(2)}, u32[]{:S(2)}) collective-permute-start(bf16[4,2,2,2,2,1,16,512]{7,0,6,5,4,3,2,1:T(4,128)(2,1)} %pad_maximum_fusion.14), channel_id=1, source_target_pairs={{0,1},{1,0},{2,3},{3,2},{4,5},{5,4},{6,7},{7,6},{8,9},{9,8},{10,11... | collective-permute-start | bytes 3145736 | tf_op jit(solution)/shard_map/ppermute | solution.py:34
  80.5 100.1 %collective-permute-start.14 = (bf16[1,2,2,2,2,1,64,512]{7,6,5,4,3,2,1,0:T(8,128)(2,1)}, bf16[1,2,2,2,2,1,64,512]{7,6,5,4,3,2,1,0:T(8,128)(2,1)}, u32[]{:S(2)}, u32[]{:S(2)}) collective-permute-start(bf16[1,2,2,2,2,1,64,512]{7,6,5,4,3,2,1,0:T(8,128)(2,1)} %pad_maximum_fusion.16), channel_id=1, source_target_pairs={{0,1},{1,0},{2,3},{3,2},{4,5},{5,4},{6,7},{7,6},{8,9},{9,8},{10,11... | collective-permute-start | bytes 3145736 | tf_op jit(solution)/shard_map/ppermute | solution.py:34
  89.0 77.0 %collective-permute-start.9 = (bf16[4,2,2,2,2,1,16,512]{7,0,6,5,4,3,2,1:T(4,128)(2,1)}, bf16[4,2,2,2,2,1,16,512]{7,0,6,5,4,3,2,1:T(4,128)(2,1)}, u32[]{:S(2)}, u32[]{:S(2)}) collective-permute-start(bf16[4,2,2,2,2,1,16,512]{7,0,6,5,4,3,2,1:T(4,128)(2,1)} %pad_maximum_fusion.15), channel_id=1, source_target_pairs={{0,1},{1,0},{2,3},{3,2},{4,5},{5,4},{6,7},{7,6},{8,9},{9,8},{10,11... | collective-permute-start | bytes 3145736 | tf_op jit(solution)/shard_map/ppermute | solution.py:34
  409.7 88.9 %collective-permute-start.27 = (bf16[4,2,2,160,512]{4,3,2,1,0:T(8,128)(2,1)}, bf16[4,2,2,160,512]{4,3,2,1,0:T(8,128)(2,1)}, u32[]{:S(2)}, u32[]{:S(2)}) collective-permute-start(bf16[4,2,2,160,512]{4,3,2,1,0:T(8,128)(2,1)} %pad_maximum_fusion.5), channel_id=1, source_target_pairs={{0,1},{1,0},{2,3},{3,2},{4,5},{5,4},{6,7},{7,6},{8,9},{9,8},{10,11... | collective-permute-start | bytes 7864328 | tf_op jit(solution)/shard_map/ppermute | solution.py:34
  418.1 78.6 %collective-permute-start.15 = (bf16[4,2,2,48,512]{4,3,2,1,0:T(8,128)(2,1)}, bf16[4,2,2,48,512]{4,3,2,1,0:T(8,128)(2,1)}, u32[]{:S(2)}, u32[]{:S(2)}) collective-permute-start(bf16[4,2,2,48,512]{4,3,2,1,0:T(8,128)(2,1)} %bitcast.66), channel_id=1, source_target_pairs={{0,1},{1,0},{2,3},{3,2},{4,5},{5,4},{6,7},{7,6},{8,9},{9,8},{10,11... | collective-permute-start | bytes 2359304 | tf_op jit(solution)/shard_map/ppermute | solution.py:34
  498.3 13.3 %collective-permute-start.16 = (bf16[4,2,48,512]{3,2,1,0:T(8,128)(2,1)S(1)}, bf16[4,2,48,512]{3,2,1,0:T(8,128)(2,1)S(1)}, u32[]{:S(2)}, u32[]{:S(2)}) collective-permute-start(bf16[4,2,48,512]{3,2,1,0:T(8,128)(2,1)S(1)} %bitcast.482), channel_id=1, source_target_pairs={{0,2},{1,3},{2,0},{3,1},{4,6},{5,7},{6,4},{7,5},{8,10},{9,11},{10,... | collective-permute-start | bytes 1179656 | tf_op jit(solution)/shard_map/ppermute | solution.py:34
  505.4 32.1 %collective-permute-start.28 = (bf16[4,2,160,512]{3,2,1,0:T(8,128)(2,1)S(1)}, bf16[4,2,160,512]{3,2,1,0:T(8,128)(2,1)S(1)}, u32[]{:S(2)}, u32[]{:S(2)}) collective-permute-start(bf16[4,2,160,512]{3,2,1,0:T(8,128)(2,1)S(1)} %pad_maximum_fusion.12), channel_id=1, source_target_pairs={{0,2},{1,3},{2,0},{3,1},{4,6},{5,7},{6,4},{7,5},{8,10},{9,11},{10,... | collective-permute-start | bytes 3932168 | tf_op jit(solution)/shard_map/ppermute | solution.py:34
  538.1 15.9 %collective-permute-start.29 = (bf16[4,160,512]{2,1,0:T(8,128)(2,1)S(1)}, bf16[4,160,512]{2,1,0:T(8,128)(2,1)S(1)}, u32[]{:S(2)}, u32[]{:S(2)}) collective-permute-start(bf16[4,160,512]{2,1,0:T(8,128)(2,1)S(1)} %pad_maximum_fusion.20), channel_id=1, source_target_pairs={{0,4},{1,5},{2,6},{3,7},{4,0},{5,1},{6,2},{7,3},{8,12},{9,13},{10,... | collective-permute-start | bytes 1966088 | tf_op jit(solution)/shard_map/ppermute | solution.py:34
  557.3 14.3 %collective-permute-start.31 = (bf16[160,512]{1,0:T(8,128)(2,1)}, bf16[160,512]{1,0:T(8,128)(2,1)}, u32[]{:S(2)}, u32[]{:S(2)}) collective-permute-start(bf16[160,512]{1,0:T(8,128)(2,1)} %pad_maximum_fusion.30), channel_id=1, source_target_pairs={{0,16},{1,17},{2,18},{3,19},{4,20},{5,21},{6,22},{7,23},{8,24},{9,... | collective-permute-start | bytes 491528 | tf_op jit(solution)/shard_map/ppermute | solution.py:102
  559.2 12.4 %collective-permute-start.32 = (bf16[160,512]{1,0:T(8,128)(2,1)}, bf16[160,512]{1,0:T(8,128)(2,1)}, u32[]{:S(2)}, u32[]{:S(2)}) collective-permute-start(bf16[160,512]{1,0:T(8,128)(2,1)} %pad_maximum_fusion.31), channel_id=1, source_target_pairs={{0,24},{1,25},{2,26},{3,27},{4,28},{5,29},{6,30},{7,31},{8,0},{9,1... | collective-permute-start | bytes 491528 | tf_op jit(solution)/shard_map/ppermute | solution.py:102
  563.5 26.0 %collective-permute-start.21 = (f32[4,16,512]{2,1,0:T(8,128)S(1)}, f32[4,16,512]{2,1,0:T(8,128)S(1)}, u32[]{:S(2)}, u32[]{:S(2)}) collective-permute-start(f32[4,16,512]{2,1,0:T(8,128)S(1)} %bitcast.474), channel_id=1, source_target_pairs={{24,0},{25,1},{26,2},{27,3},{28,4},{29,5},{30,6},{31,7}} | collective-permute-start | bytes 393224 | tf_op jit(solution)/shard_map/ppermute | solution.py:120
  564.8 31.1 %collective-permute-start.22 = (f32[4,16,512]{2,1,0:T(8,128)S(1)}, f32[4,16,512]{2,1,0:T(8,128)S(1)}, u32[]{:S(2)}, u32[]{:S(2)}) collective-permute-start(f32[4,16,512]{2,1,0:T(8,128)S(1)} %bitcast.475), channel_id=1, source_target_pairs={{16,0},{17,1},{18,2},{19,3},{20,4},{21,5},{22,6},{23,7}} | collective-permute-start | bytes 393224 | tf_op jit(solution)/shard_map/ppermute | solution.py:120
  566.1 29.8 %collective-permute-start.23 = (f32[4,16,512]{2,1,0:T(8,128)S(1)}, f32[4,16,512]{2,1,0:T(8,128)S(1)}, u32[]{:S(2)}, u32[]{:S(2)}) collective-permute-start(f32[4,16,512]{2,1,0:T(8,128)S(1)} %bitcast.476), channel_id=1, source_target_pairs={{8,0},{9,1},{10,2},{11,3},{12,4},{13,5},{14,6},{15,7}} | collective-permute-start | bytes 393224 | tf_op jit(solution)/shard_map/ppermute | solution.py:120
  580.8 17.4 %collective-permute-start.33 = (f32[4,16,512]{2,1,0:T(8,128)S(1)}, f32[4,16,512]{2,1,0:T(8,128)S(1)}, u32[]{:S(2)}, u32[]{:S(2)}) collective-permute-start(f32[4,16,512]{2,1,0:T(8,128)S(1)} %get-tuple-element.259), channel_id=1, source_target_pairs={{0,8},{1,9},{2,10},{3,11},{4,12},{5,13},{6,14},{7,15},{8,16},{9,17... | collective-permute-start | bytes 393224 | tf_op jit(solution)/shard_map/ppermute | solution.py:120
  595.9 14.6 %collective-permute-start.24 = (f32[1,4,4,16,512]{4,3,1,0,2:T(8,128)S(1)}, f32[1,4,4,16,512]{4,3,1,0,2:T(8,128)S(1)}, u32[]{:S(2)}, u32[]{:S(2)}) collective-permute-start(f32[1,4,4,16,512]{4,3,1,0,2:T(8,128)S(1)} %maximum_bitcast_fusion), channel_id=1, source_target_pairs={{0,4},{1,5},{2,6},{3,7},{4,0},{5,1},{6,2},{7,3}} | collective-permute-start | bytes 1572872 | tf_op jit(solution)/shard_map/ppermute | solution.py:124
  598.3 15.5 %collective-permute-start.36 = (f32[1,4,4,16,512]{4,3,1,0,2:T(8,128)S(1)}, f32[1,4,4,16,512]{4,3,1,0,2:T(8,128)S(1)}, u32[]{:S(2)}, u32[]{:S(2)}) collective-permute-start(f32[1,4,4,16,512]{4,3,1,0,2:T(8,128)S(1)} %maximum_bitcast_fusion.1), channel_id=1, source_target_pairs={{8,12},{9,13},{10,14},{11,15},{12,8},{13,9},{14,10},{15,11},{16,20... | collective-permute-start | bytes 1572872 | tf_op jit(solution)/shard_map/ppermute | solution.py:124
  611.7 62.8 %collective-permute-start.25 = (f32[2,4,4,16,512]{4,3,1,0,2:T(8,128)}, f32[2,4,4,16,512]{4,3,1,0,2:T(8,128)}, u32[]{:S(2)}, u32[]{:S(2)}) collective-permute-start(f32[2,4,4,16,512]{4,3,1,0,2:T(8,128)} %pad_maximum_fusion.17), channel_id=1, source_target_pairs={{0,2},{1,3},{2,0},{3,1},{4,6},{5,7},{6,4},{7,5}} | collective-permute-start | bytes 3145736 | tf_op jit(solution)/shard_map/ppermute | solution.py:124
  614.9 63.7 %collective-permute-start.37 = (f32[2,4,4,16,512]{4,3,1,0,2:T(8,128)}, f32[2,4,4,16,512]{4,3,1,0,2:T(8,128)}, u32[]{:S(2)}, u32[]{:S(2)}) collective-permute-start(f32[2,4,4,16,512]{4,3,1,0,2:T(8,128)} %pad_maximum_fusion.18), channel_id=1, source_target_pairs={{8,10},{9,11},{10,8},{11,9},{12,14},{13,15},{14,12},{15,13},{16,18... | collective-permute-start | bytes 3145736 | tf_op jit(solution)/shard_map/ppermute | solution.py:124
  676.4 16.1 %collective-permute-start.26 = (f32[4,4,4,16,512]{4,3,1,0,2:T(8,128)S(1)}, f32[4,4,4,16,512]{4,3,1,0,2:T(8,128)S(1)}, u32[]{:S(2)}, u32[]{:S(2)}) collective-permute-start(f32[4,4,4,16,512]{4,3,1,0,2:T(8,128)S(1)} %pad_maximum_fusion.9), channel_id=1, source_target_pairs={{0,1},{1,0},{2,3},{3,2},{4,5},{5,4},{6,7},{7,6}} | collective-permute-start | bytes 6291464 | tf_op jit(solution)/shard_map/ppermute | solution.py:124
  680.3 12.3 %collective-permute-start.38 = (f32[4,4,4,16,512]{4,3,1,0,2:T(8,128)S(1)}, f32[4,4,4,16,512]{4,3,1,0,2:T(8,128)S(1)}, u32[]{:S(2)}, u32[]{:S(2)}) collective-permute-start(f32[4,4,4,16,512]{4,3,1,0,2:T(8,128)S(1)} %pad_maximum_fusion.10), channel_id=1, source_target_pairs={{8,9},{9,8},{10,11},{11,10},{12,13},{13,12},{14,15},{15,14},{16,17... | collective-permute-start | bytes 6291464 | tf_op jit(solution)/shard_map/ppermute | solution.py:124
  (132 other events, 1250.1 us)
